TPU v7x, 256 devices: a whole 4x4x8 slice. The times are simulated.
256 devices in a mesh: hid: 32 (over x, z), tok: 8 (over y, core).
Axes of the slice: x: 4, y: 4, z: 8, core: 2. Of those that a mesh axis runs over, the one named last changes fastest.
Arguments:
- tokens: bfloat16 [2048, 12288], P('tok', 'hid'), may hold values from -6 to 6
- cotangent: bfloat16 [2048, 12288], P('tok', 'hid'), may hold values from -0.75 to 0.75
- up_tiles: bfloat16 [6, 256, 24576], P(None, None, 'hid'), may hold values from -0.15625 to 0.15625
- down_tiles: bfloat16 [6, 24576, 256], P(None, 'hid'), may hold values from -0.109375 to 0.109375
- block_index: int32 [6, 96, 2], P(None, 'hid'), may hold values from 0 to 2, as said below
- up_left: bfloat16 [12288, 256], P('hid'), may hold values from -0.0546875 to 0.0546875
- up_right: bfloat16 [256, 24576], P(None, 'hid'), may hold values from -0.375 to 0.375
- down_left: bfloat16 [24576, 256], P('hid'), may hold values from -0.0390625 to 0.0390625
- down_right: bfloat16 [256, 12288], P(None, 'hid'), may hold values from -0.375 to 0.375
Outputs:
- layer_out: bfloat16 [2048, 12288], P('tok', 'hid')
- grad_tokens: bfloat16 [2048, 12288], P('tok', 'hid')
- grad_up_tiles: bfloat16 [6, 256, 24576], P(None, 'tok', 'hid')
- grad_down_tiles: bfloat16 [6, 24576, 256], P(None, ('hid', 'tok'))
- grad_up_left: bfloat16 [12288, 256], P(('hid', 'tok'))
- grad_up_right: bfloat16 [256, 24576], P('tok', 'hid')
- grad_down_left: bfloat16 [24576, 256], P(('hid', 'tok'))
- grad_down_right: bfloat16 [256, 12288], P('tok', 'hid')
Inputs may be any that keep to these rules, and one draw needn't show every extreme that they name: `block_index`: each row names two different sub-blocks.
All inputs are finite; a program needn't handle non-finite values.
Results may differ from a plain program's by a relative error of at most 0.03.
Values may be sent and summed in bfloat16 or wider, within the bound.
No kernel may reach another device: no remote copies, remote signals or barrier semaphores. Data moves between devices by JAX's collectives and lax.ppermute only.
A program may use at most 128 MiB of HBM per device.

v0:
```python
import jax
import jax.numpy as jnp
from jax import lax
from jax.sharding import PartitionSpec as P

GELU_SCALE = 0.7978845608028654
GELU_CUBIC = 0.044715


def partner(block, axis, distance):
    count = lax.axis_size(axis)
    route = []
    for low in range(count):
        high = low | 1 << distance
        if high != low and high < count:
            route += [(low, high), (high, low)]
    return lax.ppermute(block, axis, route)


def gelu_parts(pre_act):
    inner = GELU_SCALE * (pre_act + GELU_CUBIC * pre_act * pre_act * pre_act)
    tanh_value = jnp.tanh(inner)
    value = 0.5 * pre_act * (1.0 + tanh_value)
    slope = 0.5 * (1.0 + tanh_value) + 0.5 * pre_act * (
        1.0 - tanh_value * tanh_value
    ) * GELU_SCALE * (1.0 + 3.0 * GELU_CUBIC * pre_act * pre_act)
    return (value, slope)


def on_device(
    tokens, cotangent, up_tiles, down_tiles, block_index, up_left, up_right, down_left, down_right
):
    hid_count = lax.axis_size("hid")
    level_count = hid_count.bit_length()
    position = lax.axis_index("hid")
    token_rows, feat_width = tokens.shape
    sub_width = feat_width // 3
    block_count = block_index.shape[1]
    hidden_width = up_tiles.shape[2]
    block_width = hidden_width // block_count
    select_float_values = (block_index[..., None] == jnp.arange(3, dtype=jnp.int32)).astype(
        jnp.float32
    )
    select_half_values = select_float_values.astype(jnp.bfloat16)
    up_blocks = [
        up_tiles[partition_key].reshape(2, sub_width, block_count, block_width)
        for partition_key in range(level_count)
    ]
    down_blocks = [
        down_tiles[partition_key].reshape(block_count, block_width, 2, sub_width)
        for partition_key in range(level_count)
    ]

    def partner_of(partition_key):
        if partition_key == 0:
            return position
        return jnp.bitwise_xor(position, jnp.int32(1 << partition_key - 1))

    def choose(field, partition_key):
        reshaped_tiles = field.reshape(token_rows, 3, sub_width)
        return jnp.einsum(
            "rfg,hyf->rhyg",
            reshaped_tiles,
            select_half_values[partition_key],
            preferred_element_type=jnp.float32,
        ).astype(jnp.bfloat16)

    def place(partner_pairs, partition_key):
        placed_blocks = jnp.einsum(
            "kdow,dog->kgw",
            partner_pairs,
            select_float_values[partition_key],
            precision=lax.Precision.HIGHEST,
        )
        return placed_blocks.reshape(token_rows, feat_width).astype(jnp.bfloat16)

    gathered = lax.all_gather(tokens, "hid", axis=1, tiled=True)
    feature_copies = [
        lax.dynamic_slice_in_dim(gathered, partner_of(partition_key) * feat_width, feat_width, 1)
        for partition_key in range(level_count)
    ]
    low_up = lax.psum(
        jnp.dot(tokens, up_left, preferred_element_type=jnp.float32).astype(jnp.bfloat16), "hid"
    )
    chosen_inputs = [
        choose(feature_copies[partition_key], partition_key) for partition_key in range(level_count)
    ]
    pre_act = jnp.dot(low_up, up_right, preferred_element_type=jnp.float32).reshape(
        token_rows, block_count, block_width
    )
    for partition_key in range(level_count):
        pre_act = pre_act + jnp.einsum(
            "tbjs,jsbh->tbh",
            chosen_inputs[partition_key],
            up_blocks[partition_key],
            preferred_element_type=jnp.float32,
        )
    hidden_value, slope = gelu_parts(pre_act)
    hidden_act = hidden_value.astype(jnp.bfloat16)
    hidden_flat = hidden_act.reshape(token_rows, hidden_width)
    low_down = lax.psum(
        jnp.dot(hidden_flat, down_left, preferred_element_type=jnp.float32).astype(jnp.bfloat16),
        "hid",
    )
    out_parts = [
        place(
            jnp.einsum(
                "tbh,bhjs->tbjs",
                hidden_act,
                down_blocks[partition_key],
                preferred_element_type=jnp.float32,
            ),
            partition_key,
        )
        for partition_key in range(level_count)
    ]
    output_acc = out_parts[0].astype(jnp.float32)
    for partition_key in range(1, level_count):
        output_acc = output_acc + partner(
            out_parts[partition_key], "hid", partition_key - 1
        ).astype(jnp.float32)
    layer_out = (
        output_acc + jnp.dot(low_down, down_right, preferred_element_type=jnp.float32)
    ).astype(jnp.bfloat16)
    back_down = lax.psum(
        jnp.dot(cotangent, down_right.T, preferred_element_type=jnp.float32).astype(jnp.bfloat16),
        "hid",
    )
    grad_gathered = lax.all_gather(cotangent, "hid", axis=1, tiled=True)
    grad_copies = [
        lax.dynamic_slice_in_dim(
            grad_gathered, partner_of(partition_key) * feat_width, feat_width, 1
        )
        for partition_key in range(level_count)
    ]
    chosen_grads = [
        choose(grad_copies[partition_key], partition_key) for partition_key in range(level_count)
    ]
    grad_hidden = jnp.dot(back_down, down_left.T, preferred_element_type=jnp.float32).reshape(
        token_rows, block_count, block_width
    )
    for partition_key in range(level_count):
        grad_hidden = grad_hidden + jnp.einsum(
            "tbjs,bhjs->tbh",
            chosen_grads[partition_key],
            down_blocks[partition_key],
            preferred_element_type=jnp.float32,
        )
    down_terms = jnp.stack(
        [
            jnp.einsum(
                "tbh,tbjs->bhjs",
                hidden_act,
                chosen_grads[partition_key],
                preferred_element_type=jnp.float32,
            ).reshape(hidden_width, 2 * sub_width)
            for partition_key in range(level_count)
        ]
    )
    down_left_term = jnp.dot(hidden_flat.T, back_down, preferred_element_type=jnp.float32)
    down_right_term = jnp.dot(low_down.T, cotangent, preferred_element_type=jnp.float32)
    grad_down_tiles, grad_down_left, grad_down_right = (
        lax.psum_scatter(
            down_terms.astype(jnp.bfloat16), "tok", scatter_dimension=1, tiled=True
        ).astype(jnp.float32),
        lax.psum_scatter(
            down_left_term.astype(jnp.bfloat16), "tok", scatter_dimension=0, tiled=True
        ).astype(jnp.float32),
        lax.psum_scatter(
            down_right_term.astype(jnp.bfloat16), "tok", scatter_dimension=0, tiled=True
        ).astype(jnp.float32),
    )
    grad_pre = (grad_hidden * slope).astype(jnp.bfloat16)
    grad_flat = grad_pre.reshape(token_rows, hidden_width)
    back_up = lax.psum(
        jnp.dot(grad_flat, up_right.T, preferred_element_type=jnp.float32).astype(jnp.bfloat16),
        "hid",
    )
    in_parts = [
        place(
            jnp.einsum(
                "tbh,jsbh->tbjs",
                grad_pre,
                up_blocks[partition_key],
                preferred_element_type=jnp.float32,
            ),
            partition_key,
        )
        for partition_key in range(level_count)
    ]
    input_acc = in_parts[0].astype(jnp.float32)
    for partition_key in range(1, level_count):
        input_acc = input_acc + partner(in_parts[partition_key], "hid", partition_key - 1).astype(
            jnp.float32
        )
    grad_tokens = (
        input_acc + jnp.dot(back_up, up_left.T, preferred_element_type=jnp.float32)
    ).astype(jnp.bfloat16)
    up_terms = jnp.stack(
        [
            jnp.einsum(
                "tbjs,tbh->jsbh",
                chosen_inputs[partition_key],
                grad_pre,
                preferred_element_type=jnp.float32,
            ).reshape(2 * sub_width, hidden_width)
            for partition_key in range(level_count)
        ]
    )
    up_right_term = jnp.dot(low_up.T, grad_flat, preferred_element_type=jnp.float32)
    up_left_term = jnp.dot(tokens.T, back_up, preferred_element_type=jnp.float32)
    grad_up_tiles, grad_up_right, grad_up_left = (
        lax.psum_scatter(
            up_terms.astype(jnp.bfloat16), "tok", scatter_dimension=1, tiled=True
        ).astype(jnp.float32),
        lax.psum_scatter(
            up_right_term.astype(jnp.bfloat16), "tok", scatter_dimension=0, tiled=True
        ).astype(jnp.float32),
        lax.psum_scatter(
            up_left_term.astype(jnp.bfloat16), "tok", scatter_dimension=0, tiled=True
        ).astype(jnp.float32),
    )
    return (
        layer_out,
        grad_tokens,
        grad_up_tiles.astype(jnp.bfloat16),
        grad_down_tiles.astype(jnp.bfloat16),
        grad_up_left.astype(jnp.bfloat16),
        grad_up_right.astype(jnp.bfloat16),
        grad_down_left.astype(jnp.bfloat16),
        grad_down_right.astype(jnp.bfloat16),
    )


def solution(mesh):
    return jax.shard_map(
        on_device,
        mesh=mesh,
        in_specs=(
            P("tok", "hid"),
            P("tok", "hid"),
            P(None, None, "hid"),
            P(None, "hid", None),
            P(None, "hid", None),
            P("hid", None),
            P(None, "hid"),
            P("hid", None),
            P(None, "hid"),
        ),
        out_specs=(
            P("tok", "hid"),
            P("tok", "hid"),
            P(None, "tok", "hid"),
            P(None, ("hid", "tok"), None),
            P(("hid", "tok"), None),
            P("tok", "hid"),
            P(("hid", "tok"), None),
            P("tok", "hid"),
        ),
        check_vma=False,
    )
```

profile of v0, /device:TPU:2, one launch (start us, length us, event | category | flops | bytes accessed | tf_op | source)
XLA Modules:
  0.0 776.2 jit_solution(9446525643140161980)
XLA Ops:
  7.3 2.1 convolution_convert_fusion.29
  16.3 2.2 reshape.191
  18.5 2.1 reshape.190
  20.6 2.3 reshape.189
  25.1 2.5 fusion.172
  30.7 127.4 %all-reduce.7.cloned.1.call-done = (bf16[256,256]{1,0:T(8,128)(2,1)}, bf16[256,256]{1,0:T(8,128)(2,1)}) async-done(((bf16[256,256]{1,0:T(8,128)(2,1)}, bf16[256,256]{1,0:T(8,128)(2,1)}), (bf16[256,256]{1,0:T(8,128)(2,1)}, bf16[256,256]{1,0:T(8,128)(2,1)})) %all-reduce.7.cloned.1.call-update) | async-done | bytes 262160 | tf_op jit(solution)/shard_map/psum | solution.py:82
  158.1 2.1 fusion.175
  160.2 2.2 fusion.176
  162.5 84.4 %all-gather.3.cloned.1.call-done = bf16[256,12288]{0,1:T(8,128)(2,1)} async-done(((bf16[256,384]{0,1:T(8,128)(2,1)}), bf16[256,12288]{0,1:T(8,128)(2,1)}) %all-gather.3.cloned.1.call-update) | async-done | bytes 6291472 | tf_op jit(solution)/shard_map/all_gather | solution.py:77
  246.9 88.8 %all-gather.5.cloned.1.call-done = bf16[256,12288]{0,1:T(8,128)(2,1)} async-done(((bf16[256,384]{0,1:T(8,128)(2,1)}), bf16[256,12288]{0,1:T(8,128)(2,1)}) %all-gather.5.cloned.1.call-update) | async-done | bytes 6291472 | tf_op jit(solution)/shard_map/all_gather | solution.py:129
  335.7 3.0 constant_dynamic-slice_fusion.5
  349.8 2.0 fusion.14
  351.8 2.0 fusion.20
  355.7 2.1 fusion.15
  357.7 2.0 fusion.21
  361.6 2.1 fusion.16
  363.7 2.1 fusion.22
  367.6 2.1 fusion.17
  369.7 2.1 fusion.23
  373.6 2.0 fusion.18
  375.6 2.1 fusion.24
  400.2 2.1 copy.346
  404.6 2.0 convolution_convert_fusion.30
  413.9 4.9 copy.351
  423.4 2.1 fusion.52
  426.2 124.4 %all-reduce.5.cloned.1.call-done = (bf16[256,256]{1,0:T(8,128)(2,1)}, bf16[256,256]{1,0:T(8,128)(2,1)}) async-done(((bf16[256,256]{1,0:T(8,128)(2,1)}, bf16[256,256]{1,0:T(8,128)(2,1)}), (bf16[256,256]{1,0:T(8,128)(2,1)}, bf16[256,256]{1,0:T(8,128)(2,1)})) %all-reduce.5.cloned.1.call-update) | async-done | bytes 262160 | tf_op jit(solution)/shard_map/psum | solution.py:101
  554.2 2.1 convolution_convert_fusion.15
  558.2 2.0 convolution_convert_fusion.13
  560.2 2.2 fusion.36
  562.7 2.1 convolution_convert_fusion.14
  569.3 2.2 copy.359
  571.6 2.0 stack_reshape.57
  573.6 2.2 copy.361
  575.8 2.0 stack_reshape.58
  577.8 2.2 copy.363
  580.0 2.0 stack_reshape.59
  583.0 2.0 copy.314
  591.1 2.1 collective-permute-start.6
  593.2 1.9 convolution_convert_fusion.12
  595.5 2.1 fusion.50
  599.6 2.5 collective-permute-start.7
  633.9 3.1 collective-permute-start.2
  639.6 2.1 add_convert_fusion
  641.7 4.1 collective-permute-done.1
  649.2 10.5 %reduce-scatter.17.cloned.1.call-done = bf16[32,384]{1,0:T(8,128)(2,1)} async-done(((bf16[256,384]{1,0:T(8,128)(2,1)}), bf16[32,384]{1,0:T(8,128)(2,1)}) %reduce-scatter.17.cloned.1.call-update) | async-done | bytes 24592 | tf_op jit(solution)/shard_map/reduce_scatter | solution.py:169
  659.8 35.3 %reduce-scatter.13.cloned.1.call-done = bf16[32,768]{1,0:T(8,128)(2,1)} async-done(((bf16[256,768]{1,0:T(8,128)(2,1)}), bf16[32,768]{1,0:T(8,128)(2,1)}) %reduce-scatter.13.cloned.1.call-update) | async-done | bytes 49168 | tf_op jit(solution)/shard_map/reduce_scatter | solution.py:216
  695.0 35.5 %reduce-scatter.15.cloned.1.call-done = bf16[96,256]{1,0:T(8,128)(2,1)} async-done(((bf16[768,256]{1,0:T(8,128)(2,1)}), bf16[96,256]{1,0:T(8,128)(2,1)}) %reduce-scatter.15.cloned.1.call-update) | async-done | bytes 49168 | tf_op jit(solution)/shard_map/reduce_scatter | solution.py:166
  730.5 38.6 %reduce-scatter.11.cloned.1.call-done = bf16[6,96,256]{2,1,0:T(8,128)(2,1)} async-done(((bf16[6,768,256]{2,1,0:T(8,128)(2,1)}), bf16[6,96,256]{2,1,0:T(8,128)(2,1)}) %reduce-scatter.11.cloned.1.call-update) | async-done | bytes 294928 | tf_op jit(solution)/shard_map/reduce_scatter | solution.py:163
  (289 shorter events, 124.5 us)
Async XLA Ops:
  7.2 150.9 %copy-start = (bf16[256,768]{1,0:T(8,128)(2,1)S(1)}, bf16[256,768]{1,0:T(8,128)(2,1)}, u32[]{:S(2)}) copy-start(bf16[256,768]{1,0:T(8,128)(2,1)} %param.15) | copy-start | bytes 1179652
  7.2 7.8 %copy-start.57 = (s32[6,3,2]{0,2,1:T(2,128)S(1)}, s32[6,3,2]{0,2,1:T(2,128)}, u32[]{:S(2)}) copy-start(s32[6,3,2]{0,2,1:T(2,128)} %param.13) | copy-start | bytes 436
  7.2 7.9 %copy-start.37 = (bf16[6,256,768]{2,1,0:T(8,128)(2,1)S(1)}, bf16[6,256,768]{2,1,0:T(8,128)(2,1)}, u32[]{:S(2)}) copy-start(bf16[6,256,768]{2,1,0:T(8,128)(2,1)} %param.11) | copy-start | bytes 7077892
  7.2 150.9 %all-reduce.7.cloned.1.call-start = ((), (), s32[]{:S(2)}) async-start(), calls=%async_computation.15 | async-start | bytes 524288 | tf_op jit(solution)/shard_map/psum | solution.py:82
  11.3 235.6 %all-gather.3.cloned.1.call-start = ((), (), s32[]{:S(2)}) async-start(), calls=%async_computation.6 | async-start | bytes 6488064 | tf_op jit(solution)/shard_map/all_gather | solution.py:77
  13.1 322.6 %all-gather.5.cloned.1.call-start = ((), (), s32[]{:S(2)}) async-start(), calls=%async_computation.7 | async-start | bytes 6488064 | tf_op jit(solution)/shard_map/all_gather | solution.py:129
  14.9 535.6 %all-reduce.5.cloned.1.call-start = ((), (), s32[]{:S(2)}) async-start(), calls=%async_computation.14 | async-start | bytes 524288 | tf_op jit(solution)/shard_map/psum | solution.py:101
  16.3 6.6 copy-start.41
  23.1 360.5 %copy-start.10 = (bf16[2,128,3,256]{3,2,1,0:T(4,128)(2,1)}, bf16[2,128,3,256]{3,2,1,0:T(4,128)(2,1)S(1)}, u32[]{:S(2)}) copy-start(bf16[2,128,3,256]{3,2,1,0:T(4,128)(2,1)S(1)} %reshape.192) | copy-start | bytes 1179652
  27.9 356.9 %copy-start.2 = (bf16[3,256,2,128]{3,2,1,0:T(2,128)(2,1)}, bf16[3,256,2,128]{3,2,1,0:T(2,128)(2,1)S(1)}, u32[]{:S(2)}) copy-start(bf16[3,256,2,128]{3,2,1,0:T(2,128)(2,1)S(1)} %reshape_squeeze.46) | copy-start | bytes 1179652
  28.0 357.1 %copy-start.4 = (bf16[3,256,2,128]{3,2,1,0:T(2,128)(2,1)}, bf16[3,256,2,128]{3,2,1,0:T(2,128)(2,1)S(1)}, u32[]{:S(2)}) copy-start(bf16[3,256,2,128]{3,2,1,0:T(2,128)(2,1)S(1)} %reshape_squeeze.45) | copy-start | bytes 1179652
  28.1 357.4 %copy-start.6 = (bf16[3,256,2,128]{3,2,1,0:T(2,128)(2,1)}, bf16[3,256,2,128]{3,2,1,0:T(2,128)(2,1)S(1)}, u32[]{:S(2)}) copy-start(bf16[3,256,2,128]{3,2,1,0:T(2,128)(2,1)S(1)} %reshape_squeeze.44) | copy-start | bytes 1179652
  28.2 357.7 %copy-start.8 = (bf16[3,256,2,128]{3,2,1,0:T(2,128)(2,1)}, bf16[3,256,2,128]{3,2,1,0:T(2,128)(2,1)S(1)}, u32[]{:S(2)}) copy-start(bf16[3,256,2,128]{3,2,1,0:T(2,128)(2,1)S(1)} %reshape_squeeze.43) | copy-start | bytes 1179652
  359.8 13.8 %copy-start.56 = (bf16[3,2,3,1]{2,1,0,3:T(2,128)(2,1)S(1)}, bf16[3,2,3,1]{2,1,0,3:T(2,128)(2,1)}, u32[]{:S(2)}) copy-start(bf16[3,2,3,1]{2,1,0,3:T(2,128)(2,1)} %get-tuple-element.77) | copy-start | bytes 112
  365.8 13.7 %copy-start.55 = (bf16[3,2,3,1]{2,1,0,3:T(2,128)(2,1)S(1)}, bf16[3,2,3,1]{2,1,0,3:T(2,128)(2,1)}, u32[]{:S(2)}) copy-start(bf16[3,2,3,1]{2,1,0,3:T(2,128)(2,1)} %get-tuple-element.76) | copy-start | bytes 112
  404.6 5.4 copy-start.48
  409.2 238.3 %reduce-scatter.9.cloned.1.call-start = ((), (), s32[]{:S(2)}) async-start(), calls=%async_computation.8 | async-start | bytes 3538944 | tf_op jit(solution)/shard_map/reduce_scatter | solution.py:213
  418.8 230.4 %reduce-scatter.19.cloned.1.call-start = ((), (), s32[]{:S(2)}) async-start(), calls=%async_computation.13 | async-start | bytes 221184
  423.4 127.2 %copy-start.39 = (bf16[256,384]{1,0:T(8,128)(2,1)S(1)}, bf16[256,384]{1,0:T(8,128)(2,1)}, u32[]{:S(2)}) copy-start(bf16[256,384]{1,0:T(8,128)(2,1)} %param.9) | copy-start | bytes 589828
  425.5 130.8 %copy-start.40 = (bf16[256,384]{1,0:T(8,128)(2,1)S(1)}, bf16[256,384]{1,0:T(8,128)(2,1)}, u32[]{:S(2)}) copy-start(bf16[256,384]{1,0:T(8,128)(2,1)} %param.10) | copy-start | bytes 589828
  554.1 105.6 %reduce-scatter.17.cloned.1.call-start = ((), (), s32[]{:S(2)}) async-start(), calls=%async_computation.12 | async-start | bytes 221184 | tf_op jit(solution)/shard_map/reduce_scatter | solution.py:169
  558.2 6.7 copy-start.47
  558.2 136.9 %reduce-scatter.13.cloned.1.call-start = ((), (), s32[]{:S(2)}) async-start(), calls=%async_computation.10 | async-start | bytes 442368 | tf_op jit(solution)/shard_map/reduce_scatter | solution.py:216
  562.5 5.4 copy-start.46
  562.5 168.0 %reduce-scatter.15.cloned.1.call-start = ((), (), s32[]{:S(2)}) async-start(), calls=%async_computation.11 | async-start | bytes 442368 | tf_op jit(solution)/shard_map/reduce_scatter | solution.py:166
  569.3 12.7 %copy-start.38 = (f32[256,3,128]{2,1,0:T(4,128)S(1)}, f32[256,3,128]{2,1,0:T(4,128)}, u32[]{:S(2)}) copy-start(f32[256,3,128]{2,1,0:T(4,128)} %fusion.36) | copy-start | bytes 1179652
  573.6 11.4 %copy-start.50 = (bf16[256,3,128]{2,1,0:T(4,128)(2,1)S(1)}, bf16[256,3,128]{2,1,0:T(4,128)(2,1)}, u32[]{:S(2)}) copy-start(bf16[256,3,128]{2,1,0:T(4,128)(2,1)} %fusion.52) | copy-start | bytes 589828
  583.0 12.1 %copy-start.14 = (bf16[2,128,3,256]{3,2,1,0:T(4,128)(2,1)S(1)}, bf16[2,128,3,256]{3,2,1,0:T(4,128)(2,1)}, u32[]{:S(2)}) copy-start(bf16[2,128,3,256]{3,2,1,0:T(4,128)(2,1)} %reshape.190) | copy-start | bytes 1179652
  587.6 44.5 %collective-permute-start.5 = (bf16[256,384]{1,0:T(8,128)(2,1)}, bf16[256,384]{1,0:T(8,128)(2,1)}, u32[]{:S(2)}, u32[]{:S(2)}) collective-permute-start(bf16[256,384]{1,0:T(8,128)(2,1)} %copy.313), channel_id=1, source_target_pairs={{0,8},{8,0},{16,24},{24,16},{32,40},{40,32},{48,56},{56,48},{64,72... | collective-permute-start | bytes 589832 | tf_op jit(solution)/shard_map/ppermute | solution.py:17
  591.1 41.5 %collective-permute-start.6 = (bf16[256,384]{1,0:T(8,128)(2,1)}, bf16[256,384]{1,0:T(8,128)(2,1)}, u32[]{:S(2)}, u32[]{:S(2)}) collective-permute-start(bf16[256,384]{1,0:T(8,128)(2,1)} %copy.320), channel_id=1, source_target_pairs={{0,16},{16,0},{8,24},{24,8},{32,48},{48,32},{40,56},{56,40},{64,80... | collective-permute-start | bytes 589832 | tf_op jit(solution)/shard_map/ppermute | solution.py:17
  595.4 7.5 copy-start.42
  595.4 8.3 %copy-start.43 = (bf16[1,768,256]{2,1,0:T(8,128)(2,1)S(1)}, bf16[1,768,256]{2,1,0:T(8,128)(2,1)}, u32[]{:S(2)}) copy-start(bf16[1,768,256]{2,1,0:T(8,128)(2,1)} %stack_reshape.56) | copy-start | bytes 1179652
  595.4 173.7 %reduce-scatter.11.cloned.1.call-start = ((), (), s32[]{:S(2)}) async-start(), calls=%async_computation.9 | async-start | bytes 2654208 | tf_op jit(solution)/shard_map/reduce_scatter | solution.py:163
  599.6 5.7 copy-start.45
  599.6 34.3 %collective-permute-start.7 = (bf16[256,384]{1,0:T(8,128)(2,1)}, bf16[256,384]{1,0:T(8,128)(2,1)}, u32[]{:S(2)}, u32[]{:S(2)}) collective-permute-start(bf16[256,384]{1,0:T(8,128)(2,1)} %copy.326), channel_id=1, source_target_pairs={{0,32},{32,0},{8,40},{40,8},{16,48},{48,16},{24,56},{56,24},{64,96... | collective-permute-start | bytes 589832 | tf_op jit(solution)/shard_map/ppermute | solution.py:17
  610.0 26.9 %collective-permute-start.8 = (bf16[256,384]{1,0:T(8,128)(2,1)S(1)}, bf16[256,384]{1,0:T(8,128)(2,1)S(1)}, u32[]{:S(2)}, u32[]{:S(2)}) collective-permute-start(bf16[256,384]{1,0:T(8,128)(2,1)S(1)} %copy.332), channel_id=1, source_target_pairs={{0,64},{64,0},{8,72},{72,8},{16,80},{80,16},{24,88},{88,24},{32,96... | collective-permute-start | bytes 589832 | tf_op jit(solution)/shard_map/ppermute | solution.py:17
  614.6 24.2 %collective-permute-start.9 = (bf16[256,384]{1,0:T(8,128)(2,1)}, bf16[256,384]{1,0:T(8,128)(2,1)S(1)}, u32[]{:S(2)}, u32[]{:S(2)}) collective-permute-start(bf16[256,384]{1,0:T(8,128)(2,1)} %copy.338), channel_id=1, source_target_pairs={{0,128},{128,0},{8,136},{136,8},{16,144},{144,16},{24,152},{152,24... | collective-permute-start | bytes 589832 | tf_op jit(solution)/shard_map/ppermute | solution.py:17
  628.2 11.4 %copy-start.49 = (f32[256,384]{1,0:T(8,128)S(1)}, f32[256,384]{1,0:T(8,128)}, u32[]{:S(2)}) copy-start(f32[256,384]{1,0:T(8,128)} %copy.314) | copy-start | bytes 1179652
  628.2 11.4 %copy-start.51 = (bf16[384,256]{1,0:T(8,128)(2,1)S(1)}, bf16[384,256]{1,0:T(8,128)(2,1)}, u32[]{:S(2)}) copy-start(bf16[384,256]{1,0:T(8,128)(2,1)} %param.14) | copy-start | bytes 589828
  628.2 11.4 %copy-start.54 = (bf16[256,256]{1,0:T(8,128)(2,1)S(1)}, bf16[256,256]{1,0:T(8,128)(2,1)}, u32[]{:S(2)}) copy-start(bf16[256,256]{1,0:T(8,128)(2,1)} %get-tuple-element.33) | copy-start | bytes 393220
  629.5 17.0 %copy-start.52 = (bf16[256,384]{1,0:T(8,128)(2,1)S(1)}, bf16[256,384]{1,0:T(8,128)(2,1)}, u32[]{:S(2)}) copy-start(bf16[256,384]{1,0:T(8,128)(2,1)} %param.17) | copy-start | bytes 589828
  629.6 17.0 %copy-start.53 = (bf16[256,256]{1,0:T(8,128)(2,1)S(1)}, bf16[256,256]{1,0:T(8,128)(2,1)}, u32[]{:S(2)}) copy-start(bf16[256,256]{1,0:T(8,128)(2,1)} %get-tuple-element.32) | copy-start | bytes 393220
  631.2 137.9 %copy-start.1 = (bf16[256,768]{1,0:T(8,128)(2,1)S(1)}, bf16[256,768]{1,0:T(8,128)(2,1)}, u32[]{:S(2)}) copy-start(bf16[256,768]{1,0:T(8,128)(2,1)} %param.15) | copy-start | bytes 1179652
  632.0 9.7 %collective-permute-start = (bf16[256,384]{1,0:T(8,128)(2,1)}, bf16[256,384]{1,0:T(8,128)(2,1)S(1)}, u32[]{:S(2)}, u32[]{:S(2)}) collective-permute-start(bf16[256,384]{1,0:T(8,128)(2,1)} %copy.251), channel_id=1, source_target_pairs={{0,8},{8,0},{16,24},{24,16},{32,40},{40,32},{48,56},{56,48},{64,72... | collective-permute-start | bytes 589832 | tf_op jit(solution)/shard_map/ppermute | solution.py:17
  632.6 13.2 %collective-permute-start.1 = (bf16[256,384]{1,0:T(8,128)(2,1)}, bf16[256,384]{1,0:T(8,128)(2,1)S(1)}, u32[]{:S(2)}, u32[]{:S(2)}) collective-permute-start(bf16[256,384]{1,0:T(8,128)(2,1)} %copy.258), channel_id=1, source_target_pairs={{0,16},{16,0},{8,24},{24,8},{32,48},{48,32},{40,56},{56,40},{64,80... | collective-permute-start | bytes 589832 | tf_op jit(solution)/shard_map/ppermute | solution.py:17
  633.9 12.6 %collective-permute-start.2 = (bf16[256,384]{1,0:T(8,128)(2,1)}, bf16[256,384]{1,0:T(8,128)(2,1)S(1)}, u32[]{:S(2)}, u32[]{:S(2)}) collective-permute-start(bf16[256,384]{1,0:T(8,128)(2,1)} %copy.264), channel_id=1, source_target_pairs={{0,32},{32,0},{8,40},{40,8},{16,48},{48,16},{24,56},{56,24},{64,96... | collective-permute-start | bytes 589832 | tf_op jit(solution)/shard_map/ppermute | solution.py:17
  637.0 9.6 %collective-permute-start.3 = (bf16[256,384]{1,0:T(8,128)(2,1)}, bf16[256,384]{1,0:T(8,128)(2,1)S(1)}, u32[]{:S(2)}, u32[]{:S(2)}) collective-permute-start(bf16[256,384]{1,0:T(8,128)(2,1)} %copy.270), channel_id=1, source_target_pairs={{0,64},{64,0},{8,72},{72,8},{16,80},{80,16},{24,88},{88,24},{32,96... | collective-permute-start | bytes 589832 | tf_op jit(solution)/shard_map/ppermute | solution.py:17
  638.7 7.8 %collective-permute-start.4 = (bf16[256,384]{1,0:T(8,128)(2,1)}, bf16[256,384]{1,0:T(8,128)(2,1)S(1)}, u32[]{:S(2)}, u32[]{:S(2)}) collective-permute-start(bf16[256,384]{1,0:T(8,128)(2,1)} %copy.276), channel_id=1, source_target_pairs={{0,128},{128,0},{8,136},{136,8},{16,144},{144,16},{24,152},{152,24... | collective-permute-start | bytes 589832 | tf_op jit(solution)/shard_map/ppermute | solution.py:17
  (30 other events, 78.4 us)
Sparse Core Ops, SparseCore 0:
  12.1 145.9 all-reduce.6
  161.3 85.5 all-gather.2
  250.0 85.6 all-gather.4
  409.3 141.2 all-reduce.4
  552.9 36.3 reduce-scatter.8
  592.3 32.1 reduce-scatter.18
  627.7 32.0 reduce-scatter.16
  662.8 32.1 reduce-scatter.12
  698.3 32.1 reduce-scatter.14
  733.5 35.5 reduce-scatter.10
where the time goes:
time: 781 us; the launch traced here: 776 us
  waiting for transfers between devices  550 us (70%)
  local copies, waits for them, and re-layouts  106 us (14%)
  matrix products  87.5 us (11%)
  starting transfers between devices  17 us (2%)
  between operations  15.4 us (2%)
    psum x1, waiting for transfers between devices, on_device(): lax.psum(jnp.dot(tokens, up_left, preferred_element_type=jnp.float32).ast...  127 us
    psum x1, waiting for transfers between devices, on_device(): lax.psum(jnp.dot(hidden_flat, down_left, preferred_element_type=jnp.float...  124 us
    all_gather x1, waiting for transfers between devices, on_device(): grad_gathered = lax.all_gather(cotangent, 'hid', axis=1, tiled=True)  88.8 us
    all_gather x1, waiting for transfers between devices, on_device(): gathered = lax.all_gather(tokens, 'hid', axis=1, tiled=True)  84.4 us
    reduce_scatter x1, waiting for transfers between devices, on_device(): lax.psum_scatter(down_terms.astype(jnp.bfloat16), 'tok', scatter_dimensio...  38.6 us
    reduce_scatter x1, waiting for transfers between devices, on_device(): lax.psum_scatter(down_left_term.astype(jnp.bfloat16), 'tok', scatter_dime...  35.5 us
    reduce_scatter x1, waiting for transfers between devices, on_device(): lax.psum_scatter(up_right_term.astype(jnp.bfloat16), 'tok', scatter_dimen...  35.3 us
    dot_general x12, matrix products, choose(): jnp.einsum('rfg,hyf->rhyg', reshaped_tiles, select_half_values[partition_...  22.3 us
  transfers between devices with their start and end apart: 20, of which 10 were waited for; matrix products, arithmetic and copies ran while one was open for 15% of the time, Pallas kernels for 0%

commit v1 on v0

--- a/solution.py
+++ b/solution.py
@@ -98,9 +98,14 @@
     hidden_value, slope = gelu_parts(pre_act)
     hidden_act = hidden_value.astype(jnp.bfloat16)
     hidden_flat = hidden_act.reshape(token_rows, hidden_width)
-    low_down = lax.psum(
-        jnp.dot(hidden_flat, down_left, preferred_element_type=jnp.float32).astype(jnp.bfloat16),
-        "hid",
+    low_down = jnp.sum(
+        lax.all_gather(
+            jnp.dot(hidden_flat, down_left, preferred_element_type=jnp.float32).astype(
+                jnp.bfloat16
+            ),
+            "hid",
+        ),
+        axis=0,
     )
     out_parts = [
         place(

time: 781 us -> 852 us (1.091)
  waiting for transfers between devices: 550 us -> 614 us
  starting transfers between devices: 17 us -> 29.4 us
  matrix products: 87.5 us -> 77.8 us
    unnamed x11 -> x12, waiting for transfers between devices: 0.17 us -> 31.6 us
    psum x1, waiting for transfers between devices: 124 us -> 99.4 us  [on_device(): lax.psum(jnp.dot(grad_flat, up_right.T, preferred_element_type=jnp.float3...]
    reduce_scatter x1, waiting for transfers between devices: 0.01 us -> 24.6 us  [on_device(): lax.psum_scatter(up_terms.astype(jnp.bfloat16), 'tok', scatter_dimension=...]
    reduce_scatter x1, waiting for transfers between devices: 10.5 us -> 35 us  [on_device(): lax.psum_scatter(down_right_term.astype(jnp.bfloat16), 'tok', scatter_dim...]
    reduce_scatter x1, starting transfers between devices: 0.04 us -> 11.5 us  [on_device(): lax.psum_scatter(up_right_term.astype(jnp.bfloat16), 'tok', scatter_dimen...]
    all_gather x0 -> x1, waiting for transfers between devices: none -> 10.7 us  [on_device(): lax.all_gather(jnp.dot(hidden_flat, down_left, preferred_element_type=jnp...]
    unnamed x131 -> x139, local copies, waits for them, and re-layouts: 17.7 us -> 18.9 us
  transfers between devices with their start and end apart: 20 -> 21, of which waited for: 10 -> 11; matrix products, arithmetic and copies ran while one was open for 15% -> 15% of each run, Pallas kernels for 0% -> 0%
where the time goes in v1:
time: 852 us; the launch traced here: 841 us
  waiting for transfers between devices  614 us (72%)
  local copies, waits for them, and re-layouts  101 us (12%)
  matrix products  77.8 us (9%)
  starting transfers between devices  29.4 us (3%)
  between operations  15.4 us (2%)
    psum x1, waiting for transfers between devices, on_device(): lax.psum(jnp.dot(tokens, up_left, preferred_element_type=jnp.float32).ast...  131 us
    psum x1, waiting for transfers between devices, on_device(): lax.psum(jnp.dot(grad_flat, up_right.T, preferred_element_type=jnp.float3...  99.4 us
    all_gather x1, waiting for transfers between devices, on_device(): grad_gathered = lax.all_gather(cotangent, 'hid', axis=1, tiled=True)  88.8 us
    all_gather x1, waiting for transfers between devices, on_device(): gathered = lax.all_gather(tokens, 'hid', axis=1, tiled=True)  84.4 us
    reduce_scatter x1, waiting for transfers between devices, on_device(): lax.psum_scatter(down_terms.astype(jnp.bfloat16), 'tok', scatter_dimensio...  38.6 us
    reduce_scatter x1, waiting for transfers between devices, on_device(): lax.psum_scatter(down_left_term.astype(jnp.bfloat16), 'tok', scatter_dime...  35.4 us
    reduce_scatter x1, waiting for transfers between devices, on_device(): lax.psum_scatter(up_right_term.astype(jnp.bfloat16), 'tok', scatter_dimen...  35.2 us
    reduce_scatter x1, waiting for transfers between devices, on_device(): lax.psum_scatter(down_right_term.astype(jnp.bfloat16), 'tok', scatter_dim...  35 us
  transfers between devices with their start and end apart: 21, of which 11 were waited for; matrix products, arithmetic and copies ran while one was open for 15% of the time, Pallas kernels for 0%

profile of v1, /device:TPU:2, one launch (start us, length us, event | category | flops | bytes accessed | tf_op | source)
XLA Modules:
  0.0 841.1 jit_solution(6058491705306170514)
XLA Ops:
  7.2 2.0 convolution_convert_fusion.29
  9.2 1.9 convolution_convert_fusion.31
  21.8 2.5 fusion.172
  27.4 130.7 %all-reduce.6.cloned.1.call-done = (bf16[256,256]{1,0:T(8,128)(2,1)}, bf16[256,256]{1,0:T(8,128)(2,1)}) async-done(((bf16[256,256]{1,0:T(8,128)(2,1)}, bf16[256,256]{1,0:T(8,128)(2,1)}), (bf16[256,256]{1,0:T(8,128)(2,1)}, bf16[256,256]{1,0:T(8,128)(2,1)})) %all-reduce.6.cloned.1.call-update) | async-done | bytes 262160 | tf_op jit(solution)/shard_map/psum | solution.py:82
  158.1 2.1 fusion.175
  160.2 2.3 fusion.176
  162.4 84.4 %all-gather.5.cloned.1.call-done = bf16[256,12288]{0,1:T(8,128)(2,1)} async-done(((bf16[256,384]{0,1:T(8,128)(2,1)}), bf16[256,12288]{0,1:T(8,128)(2,1)}) %all-gather.5.cloned.1.call-update) | async-done | bytes 6291472 | tf_op jit(solution)/shard_map/all_gather | solution.py:77
  246.8 88.8 %all-gather.7.cloned.1.call-done = bf16[256,12288]{0,1:T(8,128)(2,1)} async-done(((bf16[256,384]{0,1:T(8,128)(2,1)}), bf16[256,12288]{0,1:T(8,128)(2,1)}) %all-gather.7.cloned.1.call-update) | async-done | bytes 6291472 | tf_op jit(solution)/shard_map/all_gather | solution.py:134
  335.7 3.0 constant_dynamic-slice_fusion.5
  349.7 2.0 fusion.14
  351.7 2.1 fusion.20
  355.6 2.1 fusion.15
  357.7 2.0 fusion.21
  359.7 1.8 copy.288
  361.5 2.1 fusion.16
  363.6 2.1 fusion.22
  365.7 1.8 copy.292
  367.5 2.1 fusion.17
  369.6 2.1 fusion.23
  373.5 2.0 fusion.18
  375.5 2.0 fusion.24
  390.2 2.0 convolution_convert_fusion.30
  396.4 2.0 stack_reshape.49
  399.9 2.0 stack_reshape.50
  403.3 2.1 stack_reshape.51
  406.8 2.0 stack_reshape.52
  410.3 2.0 stack_reshape.53
  417.0 4.9 copy.351
  429.9 99.4 %all-reduce.4.cloned.1.call-done = bf16[256,256]{1,0:T(8,128)(2,1)} async-done(((bf16[256,256]{1,0:T(8,128)(2,1)}), bf16[256,256]{1,0:T(8,128)(2,1)}) %all-reduce.4.cloned.1.call-update) | async-done | bytes 131088 | tf_op jit(solution)/shard_map/psum | solution.py:180
  531.3 11.5 %reduce-scatter.13.cloned.1.call-start = ((), (), s32[]{:S(2)}) async-start(), calls=%async_computation.11 | async-start | bytes 442368 | tf_op jit(solution)/shard_map/reduce_scatter | solution.py:221
  545.4 1.8 constant_dynamic-update-slice_fusion.11
  555.1 1.9 copy.314
  562.9 1.9 convolution_convert_fusion.12
  578.0 2.5 collective-permute-start.7
  586.1 2.5 collective-permute-start.9
  604.5 10.7 %all-gather.9.cloned.1.call-done = bf16[8192,256]{1,0:T(8,128)(2,1)} async-done(((bf16[256,256]{1,0:T(8,128)(2,1)}), bf16[8192,256]{1,0:T(8,128)(2,1)}) %all-gather.9.cloned.1.call-update) | async-done | bytes 4194320 | tf_op jit(solution)/shard_map/all_gather | solution.py:102
  615.3 2.9 reduce_sum.12
  620.5 1.9 collective-permute-start.1
  622.4 2.8 collective-permute-start.2
  626.3 2.1 collective-permute-start.4
  628.4 2.0 add_convert_fusion
  630.3 24.6 %reduce-scatter.9.cloned.1.call-done = bf16[6,32,768]{2,0,1:T(8,128)(2,1)} async-done(((bf16[6,256,768]{2,0,1:T(8,128)(2,1)}), bf16[6,32,768]{2,0,1:T(8,128)(2,1)}) %reduce-scatter.9.cloned.1.call-update) | async-done | bytes 294928 | tf_op jit(solution)/shard_map/reduce_scatter | solution.py:218
  656.7 1.8 add_convert_fusion.1
  658.6 31.4 %reduce-scatter.19.cloned.1.call-done = bf16[48,256]{1,0:T(8,128)(2,1)} async-done(((bf16[384,256]{1,0:T(8,128)(2,1)}), bf16[48,256]{1,0:T(8,128)(2,1)}) %reduce-scatter.19.cloned.1.call-update) | async-done | bytes 24592
  689.9 35.2 %reduce-scatter.13.cloned.1.call-done = bf16[32,768]{1,0:T(8,128)(2,1)} async-done(((bf16[256,768]{1,0:T(8,128)(2,1)}), bf16[32,768]{1,0:T(8,128)(2,1)}) %reduce-scatter.13.cloned.1.call-update) | async-done | bytes 49168 | tf_op jit(solution)/shard_map/reduce_scatter | solution.py:221
  725.1 35.4 %reduce-scatter.15.cloned.1.call-done = bf16[96,256]{1,0:T(8,128)(2,1)} async-done(((bf16[768,256]{1,0:T(8,128)(2,1)}), bf16[96,256]{1,0:T(8,128)(2,1)}) %reduce-scatter.15.cloned.1.call-update) | async-done | bytes 49168 | tf_op jit(solution)/shard_map/reduce_scatter | solution.py:171
  760.6 38.6 %reduce-scatter.11.cloned.1.call-done = bf16[6,96,256]{2,1,0:T(8,128)(2,1)} async-done(((bf16[6,768,256]{2,1,0:T(8,128)(2,1)}), bf16[6,96,256]{2,1,0:T(8,128)(2,1)}) %reduce-scatter.11.cloned.1.call-update) | async-done | bytes 294928 | tf_op jit(solution)/shard_map/reduce_scatter | solution.py:168
  799.2 35.0 %reduce-scatter.17.cloned.1.call-done = bf16[32,384]{1,0:T(8,128)(2,1)} async-done(((bf16[256,384]{1,0:T(8,128)(2,1)}), bf16[32,384]{1,0:T(8,128)(2,1)}) %reduce-scatter.17.cloned.1.call-update) | async-done | bytes 24592 | tf_op jit(solution)/shard_map/reduce_scatter | solution.py:174
  (301 shorter events, 121.0 us)
Async XLA Ops:
  7.2 150.9 %copy-start = (bf16[256,768]{1,0:T(8,128)(2,1)S(1)}, bf16[256,768]{1,0:T(8,128)(2,1)}, u32[]{:S(2)}) copy-start(bf16[256,768]{1,0:T(8,128)(2,1)} %param.15) | copy-start | bytes 1179652
  7.2 7.7 copy-start.61
  7.2 150.9 %all-reduce.6.cloned.1.call-start = ((), (), s32[]{:S(2)}) async-start(), calls=%async_computation.16 | async-start | bytes 524288 | tf_op jit(solution)/shard_map/psum | solution.py:82
  11.1 235.7 %all-gather.5.cloned.1.call-start = ((), (), s32[]{:S(2)}) async-start(), calls=%async_computation.6 | async-start | bytes 6488064 | tf_op jit(solution)/shard_map/all_gather | solution.py:77
  13.0 322.7 %all-gather.7.cloned.1.call-start = ((), (), s32[]{:S(2)}) async-start(), calls=%async_computation.7 | async-start | bytes 6488064 | tf_op jit(solution)/shard_map/all_gather | solution.py:134
  14.8 514.5 %all-reduce.4.cloned.1.call-start = ((), (), s32[]{:S(2)}) async-start(), calls=%async_computation.8 | async-start | bytes 262144 | tf_op jit(solution)/shard_map/psum | solution.py:180
  19.8 363.9 %copy-start.10 = (bf16[2,128,3,256]{3,2,1,0:T(4,128)(2,1)}, bf16[2,128,3,256]{3,2,1,0:T(4,128)(2,1)S(1)}, u32[]{:S(2)}) copy-start(bf16[2,128,3,256]{3,2,1,0:T(4,128)(2,1)S(1)} %reshape.193) | copy-start | bytes 1179652
  24.5 360.3 %copy-start.2 = (bf16[3,256,2,128]{3,2,1,0:T(2,128)(2,1)}, bf16[3,256,2,128]{3,2,1,0:T(2,128)(2,1)S(1)}, u32[]{:S(2)}) copy-start(bf16[3,256,2,128]{3,2,1,0:T(2,128)(2,1)S(1)} %reshape_squeeze.46) | copy-start | bytes 1179652
  24.7 360.6 %copy-start.4 = (bf16[3,256,2,128]{3,2,1,0:T(2,128)(2,1)}, bf16[3,256,2,128]{3,2,1,0:T(2,128)(2,1)S(1)}, u32[]{:S(2)}) copy-start(bf16[3,256,2,128]{3,2,1,0:T(2,128)(2,1)S(1)} %reshape_squeeze.45) | copy-start | bytes 1179652
  24.8 360.9 %copy-start.6 = (bf16[3,256,2,128]{3,2,1,0:T(2,128)(2,1)}, bf16[3,256,2,128]{3,2,1,0:T(2,128)(2,1)S(1)}, u32[]{:S(2)}) copy-start(bf16[3,256,2,128]{3,2,1,0:T(2,128)(2,1)S(1)} %reshape_squeeze.44) | copy-start | bytes 1179652
  24.9 361.1 %copy-start.8 = (bf16[3,256,2,128]{3,2,1,0:T(2,128)(2,1)}, bf16[3,256,2,128]{3,2,1,0:T(2,128)(2,1)S(1)}, u32[]{:S(2)}) copy-start(bf16[3,256,2,128]{3,2,1,0:T(2,128)(2,1)S(1)} %reshape_squeeze.43) | copy-start | bytes 1179652
  359.7 13.7 %copy-start.60 = (bf16[3,2,3,1]{2,1,0,3:T(2,128)(2,1)S(1)}, bf16[3,2,3,1]{2,1,0,3:T(2,128)(2,1)}, u32[]{:S(2)}) copy-start(bf16[3,2,3,1]{2,1,0,3:T(2,128)(2,1)} %get-tuple-element.75) | copy-start | bytes 112
  365.7 13.7 %copy-start.59 = (bf16[3,2,3,1]{2,1,0,3:T(2,128)(2,1)S(1)}, bf16[3,2,3,1]{2,1,0,3:T(2,128)(2,1)}, u32[]{:S(2)}) copy-start(bf16[3,2,3,1]{2,1,0,3:T(2,128)(2,1)} %get-tuple-element.74) | copy-start | bytes 112
  390.2 225.1 %all-gather.9.cloned.1.call-start = ((), (), s32[]{:S(2)}) async-start(), calls=%async_computation.14 | async-start | bytes 4325376 | tf_op jit(solution)/shard_map/all_gather | solution.py:102
  392.2 262.7 %reduce-scatter.9.cloned.1.call-start = ((), (), s32[]{:S(2)}) async-start(), calls=%async_computation.9 | async-start | bytes 3538944 | tf_op jit(solution)/shard_map/reduce_scatter | solution.py:218
  395.3 6.6 copy-start.38
  398.7 6.6 copy-start.39
  402.1 6.7 copy-start.41
  406.8 6.3 copy-start.47
  422.0 268.0 %reduce-scatter.19.cloned.1.call-start = ((), (), s32[]{:S(2)}) async-start(), calls=%async_computation.15 | async-start | bytes 221184
  427.8 101.5 %copy-start.44 = (bf16[256,384]{1,0:T(8,128)(2,1)S(1)}, bf16[256,384]{1,0:T(8,128)(2,1)}, u32[]{:S(2)}) copy-start(bf16[256,384]{1,0:T(8,128)(2,1)} %param.9) | copy-start | bytes 589828
  428.1 114.7 %copy-start.57 = (bf16[256,256]{1,0:T(8,128)(2,1)S(1)}, bf16[256,256]{1,0:T(8,128)(2,1)}, u32[]{:S(2)}) copy-start(bf16[256,256]{1,0:T(8,128)(2,1)} %get-tuple-element.32) | copy-start | bytes 393220
  531.3 193.9 %reduce-scatter.13.cloned.1.call-start = ((), (), s32[]{:S(2)}) async-start(), calls=%async_computation.11 | async-start | bytes 442368 | tf_op jit(solution)/shard_map/reduce_scatter | solution.py:221
  545.3 6.8 copy-start.53
  545.4 215.2 %reduce-scatter.15.cloned.1.call-start = ((), (), s32[]{:S(2)}) async-start(), calls=%async_computation.12 | async-start | bytes 442368 | tf_op jit(solution)/shard_map/reduce_scatter | solution.py:171
  547.3 6.3 copy-start.52
  554.2 10.6 %copy-start.24 = (bf16[256,3,2,128]{3,1,0,2:T(4,128)(2,1)S(1)}, bf16[256,3,2,128]{3,1,0,2:T(4,128)(2,1)}, u32[]{:S(2)}) copy-start(bf16[256,3,2,128]{3,1,0,2:T(4,128)(2,1)} %fusion.24) | copy-start | bytes 1179652
  557.0 8.9 %copy-start.46 = (bf16[1,768,256]{2,1,0:T(8,128)(2,1)S(1)}, bf16[1,768,256]{2,1,0:T(8,128)(2,1)}, u32[]{:S(2)}) copy-start(bf16[1,768,256]{2,1,0:T(8,128)(2,1)} %stack_reshape.57) | copy-start | bytes 1179652
  558.0 61.1 %collective-permute-start.5 = (bf16[256,384]{1,0:T(8,128)(2,1)}, bf16[256,384]{1,0:T(8,128)(2,1)}, u32[]{:S(2)}, u32[]{:S(2)}) collective-permute-start(bf16[256,384]{1,0:T(8,128)(2,1)} %copy.313), channel_id=1, source_target_pairs={{0,8},{8,0},{16,24},{24,16},{32,40},{40,32},{48,56},{56,48},{64,72... | collective-permute-start | bytes 589832 | tf_op jit(solution)/shard_map/ppermute | solution.py:17
  565.8 233.3 %reduce-scatter.11.cloned.1.call-start = ((), (), s32[]{:S(2)}) async-start(), calls=%async_computation.10 | async-start | bytes 2654208 | tf_op jit(solution)/shard_map/reduce_scatter | solution.py:168
  571.6 262.5 %reduce-scatter.17.cloned.1.call-start = ((), (), s32[]{:S(2)}) async-start(), calls=%async_computation.13 | async-start | bytes 221184 | tf_op jit(solution)/shard_map/reduce_scatter | solution.py:174
  573.1 7.3 copy-start.12
  574.2 46.3 %collective-permute-start.6 = (bf16[256,384]{1,0:T(8,128)(2,1)}, bf16[256,384]{1,0:T(8,128)(2,1)S(1)}, u32[]{:S(2)}, u32[]{:S(2)}) collective-permute-start(bf16[256,384]{1,0:T(8,128)(2,1)} %copy.320), channel_id=1, source_target_pairs={{0,16},{16,0},{8,24},{24,8},{32,48},{48,32},{40,56},{56,40},{64,80... | collective-permute-start | bytes 589832 | tf_op jit(solution)/shard_map/ppermute | solution.py:17
  577.0 6.3 copy-start.11
  578.0 44.4 %collective-permute-start.7 = (bf16[256,384]{1,0:T(8,128)(2,1)}, bf16[256,384]{1,0:T(8,128)(2,1)}, u32[]{:S(2)}, u32[]{:S(2)}) collective-permute-start(bf16[256,384]{1,0:T(8,128)(2,1)} %copy.326), channel_id=1, source_target_pairs={{0,32},{32,0},{8,40},{40,8},{16,48},{48,16},{24,56},{56,24},{64,96... | collective-permute-start | bytes 589832 | tf_op jit(solution)/shard_map/ppermute | solution.py:17
  582.6 42.6 %collective-permute-start.8 = (bf16[256,384]{1,0:T(8,128)(2,1)S(1)}, bf16[256,384]{1,0:T(8,128)(2,1)S(1)}, u32[]{:S(2)}, u32[]{:S(2)}) collective-permute-start(bf16[256,384]{1,0:T(8,128)(2,1)S(1)} %copy.332), channel_id=1, source_target_pairs={{0,64},{64,0},{8,72},{72,8},{16,80},{80,16},{24,88},{88,24},{32,96... | collective-permute-start | bytes 589832 | tf_op jit(solution)/shard_map/ppermute | solution.py:17
  586.1 40.2 %collective-permute-start.9 = (bf16[256,384]{1,0:T(8,128)(2,1)}, bf16[256,384]{1,0:T(8,128)(2,1)S(1)}, u32[]{:S(2)}, u32[]{:S(2)}) collective-permute-start(bf16[256,384]{1,0:T(8,128)(2,1)} %copy.338), channel_id=1, source_target_pairs={{0,128},{128,0},{8,136},{136,8},{16,144},{144,16},{24,152},{152,24... | collective-permute-start | bytes 589832 | tf_op jit(solution)/shard_map/ppermute | solution.py:17
  603.7 14.4 %copy-start.45 = (bf16[256,384]{1,0:T(8,128)(2,1)S(1)}, bf16[256,384]{1,0:T(8,128)(2,1)}, u32[]{:S(2)}) copy-start(bf16[256,384]{1,0:T(8,128)(2,1)} %param.10) | copy-start | bytes 589828
  615.3 13.1 %copy-start.54 = (f32[256,384]{1,0:T(8,128)S(1)}, f32[256,384]{1,0:T(8,128)}, u32[]{:S(2)}) copy-start(f32[256,384]{1,0:T(8,128)} %copy.314) | copy-start | bytes 1179652
  615.3 13.1 %copy-start.55 = (bf16[384,256]{1,0:T(8,128)(2,1)S(1)}, bf16[384,256]{1,0:T(8,128)(2,1)}, u32[]{:S(2)}) copy-start(bf16[384,256]{1,0:T(8,128)(2,1)} %param.14) | copy-start | bytes 589828
  615.3 13.1 %copy-start.58 = (bf16[256,256]{1,0:T(8,128)(2,1)S(1)}, bf16[256,256]{1,0:T(8,128)(2,1)}, u32[]{:S(2)}) copy-start(bf16[256,256]{1,0:T(8,128)(2,1)} %all-reduce.4.cloned.1.call-done) | copy-start | bytes 393220
  618.1 38.6 %copy-start.56 = (bf16[256,384]{1,0:T(8,128)(2,1)S(1)}, bf16[256,384]{1,0:T(8,128)(2,1)}, u32[]{:S(2)}) copy-start(bf16[256,384]{1,0:T(8,128)(2,1)} %param.17) | copy-start | bytes 589828
  618.2 216.0 %copy-start.1 = (bf16[256,768]{1,0:T(8,128)(2,1)S(1)}, bf16[256,768]{1,0:T(8,128)(2,1)}, u32[]{:S(2)}) copy-start(bf16[256,768]{1,0:T(8,128)(2,1)} %param.15) | copy-start | bytes 1179652
  619.2 37.5 %collective-permute-start = (bf16[256,384]{1,0:T(8,128)(2,1)}, bf16[256,384]{1,0:T(8,128)(2,1)S(1)}, u32[]{:S(2)}, u32[]{:S(2)}) collective-permute-start(bf16[256,384]{1,0:T(8,128)(2,1)} %copy.251), channel_id=1, source_target_pairs={{0,8},{8,0},{16,24},{24,16},{32,40},{40,32},{48,56},{56,48},{64,72... | collective-permute-start | bytes 589832 | tf_op jit(solution)/shard_map/ppermute | solution.py:17
  620.5 36.2 %collective-permute-start.1 = (bf16[256,384]{1,0:T(8,128)(2,1)}, bf16[256,384]{1,0:T(8,128)(2,1)S(1)}, u32[]{:S(2)}, u32[]{:S(2)}) collective-permute-start(bf16[256,384]{1,0:T(8,128)(2,1)} %copy.258), channel_id=1, source_target_pairs={{0,16},{16,0},{8,24},{24,8},{32,48},{48,32},{40,56},{56,40},{64,80... | collective-permute-start | bytes 589832 | tf_op jit(solution)/shard_map/ppermute | solution.py:17
  622.4 34.3 %collective-permute-start.2 = (bf16[256,384]{1,0:T(8,128)(2,1)}, bf16[256,384]{1,0:T(8,128)(2,1)S(1)}, u32[]{:S(2)}, u32[]{:S(2)}) collective-permute-start(bf16[256,384]{1,0:T(8,128)(2,1)} %copy.264), channel_id=1, source_target_pairs={{0,32},{32,0},{8,40},{40,8},{16,48},{48,16},{24,56},{56,24},{64,96... | collective-permute-start | bytes 589832 | tf_op jit(solution)/shard_map/ppermute | solution.py:17
  625.2 31.5 %collective-permute-start.3 = (bf16[256,384]{1,0:T(8,128)(2,1)}, bf16[256,384]{1,0:T(8,128)(2,1)S(1)}, u32[]{:S(2)}, u32[]{:S(2)}) collective-permute-start(bf16[256,384]{1,0:T(8,128)(2,1)} %copy.270), channel_id=1, source_target_pairs={{0,64},{64,0},{8,72},{72,8},{16,80},{80,16},{24,88},{88,24},{32,96... | collective-permute-start | bytes 589832 | tf_op jit(solution)/shard_map/ppermute | solution.py:17
  626.3 30.4 %collective-permute-start.4 = (bf16[256,384]{1,0:T(8,128)(2,1)}, bf16[256,384]{1,0:T(8,128)(2,1)}, u32[]{:S(2)}, u32[]{:S(2)}) collective-permute-start(bf16[256,384]{1,0:T(8,128)(2,1)} %copy.276), channel_id=1, source_target_pairs={{0,128},{128,0},{8,136},{136,8},{16,144},{144,16},{24,152},{152,24... | collective-permute-start | bytes 589832 | tf_op jit(solution)/shard_map/ppermute | solution.py:17
  (35 other events, 104.4 us)
Sparse Core Ops, SparseCore 0:
  12.1 145.9 all-reduce.5
  161.2 85.5 all-gather.4
  250.0 85.6 all-gather.6
  390.3 138.9 all-reduce.3
  532.0 83.1 all-gather.8
  617.8 37.0 reduce-scatter.8
  658.2 31.7 reduce-scatter.18
  693.0 32.0 reduce-scatter.12
  728.4 32.1 reduce-scatter.14
  763.6 35.5 reduce-scatter.10
  802.3 31.8 reduce-scatter.16
